TPU v7x, 32 devices: a whole 2x2x4 slice. The times are simulated.
32 devices in a mesh: dp: 4 (over x, core), tensor: 8 (over z, y).
Axes of the slice: x: 2, y: 2, z: 4, core: 2. Of those that a mesh axis runs over, the one named last changes fastest.
Arguments:
- tokens: bfloat16 [768, 4096], P('dp', 'tensor'), may hold values from -6 to 6
- tangents: bfloat16 [768, 4096], P('dp', 'tensor'), may hold values from -6 to 6
- probes: bfloat16 [768, 4096], P('dp', 'tensor'), may hold values from -0.09375 to 0.09375
- w_gate: bfloat16 [4096, 14336], P('dp', 'tensor'), may hold values from -0.09375 to 0.09375
- w_up: bfloat16 [4096, 14336], P('dp', 'tensor'), may hold values from -0.09375 to 0.09375
- w_down: bfloat16 [14336, 4096], P('tensor'), may hold values from -3 to 3
Outputs:
- grad_gate: float32 [4096, 14336], P('dp', 'tensor')
- grad_up: float32 [4096, 14336], P('dp', 'tensor')
- projection: float32 [768], P('dp')
All inputs are finite; a program needn't handle non-finite values.
Results may differ from a plain program's by a relative error of at most 0.019.
Values may be sent and summed in bfloat16 or wider, within the bound.
A program may use at most 128 MiB of HBM per device.

v0:
```python
import functools
import jax
import jax.numpy as jnp
from jax import lax
from jax.sharding import PartitionSpec as P

CORES = 2


def body(n_dp, n_tensor, pieces, tokens, tangents, probes, w_gate, w_up, w_down):
    chips = n_dp // CORES
    me = lax.axis_index("dp")
    rows = tokens.shape[0]
    depth, hidden = w_gate.shape
    f32, bf16 = (jnp.float32, jnp.bfloat16)

    def shift(value, step, flip):
        pairs = []
        for at in range(n_dp):
            chip, core = (at // CORES, at % CORES)
            pairs.append(((chip + step) % chips * CORES + (core ^ flip), at))
        return lax.ppermute(value, "dp", pairs)

    def owner(step, flip):
        return (me // CORES + step) % chips * CORES + (me % CORES ^ flip)

    both = jnp.stack([tokens, tangents], axis=0)
    full = lax.all_gather(both, "tensor", axis=2, tiled=True)
    full_probe = lax.all_gather(probes, "tensor", axis=1, tiled=True)

    def columns(at):
        return lax.dynamic_slice_in_dim(full, at * depth, depth, 2)

    blocks = [[None] * chips for _ in range(CORES)]
    for flip in range(CORES):
        for step in range(chips):
            if step == 0 and flip == 0:
                blocks[0][0] = columns(me)
            else:
                blocks[flip][step] = shift(columns(owner(-step, flip)), step, flip)
    own = jnp.stack(blocks[0], axis=1)
    far = jnp.stack(blocks[1], axis=1)
    own_rows = own.reshape(-1, depth)
    far_rows = far.reshape(-1, depth)
    readout = lax.dot_general(
        full_probe, w_down, (((1,), (1,)), ((), ())), preferred_element_type=f32
    )
    width = hidden // pieces
    projection = jnp.zeros((rows,), f32)
    gathered = []
    for piece in range(pieces):
        cut = slice(piece * width, (piece + 1) * width)
        wg, wu = (w_gate[:, cut], w_up[:, cut])

        def partial(left, weight):
            return jnp.dot(left, weight, preferred_element_type=f32).reshape(2, chips, rows, width)

        sums = []
        for weight in (wg, wu):
            there = shift(partial(far_rows, weight).astype(bf16), 0, 1)
            here = partial(own_rows, weight) + there.astype(f32)
            total = here[:, 0]
            for step in range(1, chips):
                total = total + shift(here[:, step].astype(bf16), -step, 0).astype(f32)
            sums.append(total)
        gate_val, gate_dot = (sums[0][0], sums[0][1])
        up_val, up_dot = (sums[1][0], sums[1][1])
        sg = jax.nn.sigmoid(gate_val)
        silu_val = gate_val * sg
        slope = sg * (1.0 + gate_val * (1.0 - sg))
        bend = sg * (1.0 - sg) * (2.0 + gate_val * (1.0 - 2.0 * sg))
        out = readout[:, cut]
        hidden_dot = slope * gate_dot * up_val + silu_val * up_dot
        projection = projection + jnp.sum(hidden_dot * out, axis=1)
        cot = jnp.stack(
            [
                out * (bend * gate_dot * up_val + slope * up_dot),
                out * slope * up_val,
                out * slope * gate_dot,
                out * silu_val,
            ],
            axis=0,
        ).astype(bf16)
        mine = [cot] + [shift(cot, step, 0) for step in range(1, chips)]
        partner = [shift(value, 0, 1) for value in mine]
        gathered.append(jnp.stack(mine + partner, axis=1))
    bit = 1
    while bit < n_tensor:
        pairs = [(at ^ bit, at) for at in range(n_tensor)]
        projection = projection + lax.ppermute(projection, "tensor", pairs)
        bit *= 2
    factor = jnp.stack(
        [
            projection if step == 0 and flip == 0 else shift(projection, step, flip)
            for flip in range(CORES)
            for step in range(chips)
        ]
    )
    scaled = jnp.concatenate([own, far], axis=1).astype(f32) * (2.0 * factor)[None, :, :, None]
    scaled = scaled.astype(bf16).reshape(-1, depth)
    grads = ([], [])
    for block in gathered:
        flat = block.reshape(2, -1, width)
        for at in range(2):
            grads[at].append(
                lax.dot_general(
                    scaled, flat[at], (((0,), (0,)), ((), ())), preferred_element_type=f32
                )
            )
    return (jnp.concatenate(grads[0], axis=1), jnp.concatenate(grads[1], axis=1), projection)


def solution(mesh):
    n_dp, n_tensor = (mesh.shape["dp"], mesh.shape["tensor"])
    placed = (P("dp", "tensor"),) * 5 + (P("tensor", None),)
    return jax.shard_map(
        functools.partial(body, n_dp, n_tensor, 2),
        mesh=mesh,
        in_specs=placed,
        out_specs=(P("dp", "tensor"), P("dp", "tensor"), P("dp")),
        check_vma=False,
    )
```

profile of v0, /device:TPU:5, one launch (start us, length us, event | category | flops | bytes accessed | tf_op | source)
XLA Modules:
  0.0 341.4 jit_solution(14751222555207238204)
XLA Ops:
  9.9 64.7 %all-gather.3.cloned.1.call-done = bf16[2,192,4096]{2,1,0:T(8,128)(2,1)} async-done(((bf16[2,192,512]{2,1,0:T(8,128)(2,1)}), bf16[2,192,4096]{2,1,0:T(8,128)(2,1)}) %all-gather.3.cloned.1.call-update) | async-done | bytes 3145744 | tf_op jit(solution)/shard_map/all_gather | solution.py:28
  74.6 2.5 dynamic-slice_bitcast_fusion
  78.8 18.2 %collective-permute-done.2 = bf16[2,192,1024]{2,1,0:T(8,128)(2,1)S(1)} collective-permute-done((bf16[2,192,1024]{2,1,0:T(8,128)(2,1)S(1)}, bf16[2,192,1024]{2,1,0:T(8,128)(2,1)S(1)}, u32[]{:S(2)}, u32[]{:S(2)}) %collective-permute-start.2) | collective-permute-done | bytes 786464 | tf_op jit(solution)/shard_map/ppermute | solution.py:22
  97.1 2.9 fusion.50
  100.4 18.7 %all-gather.5.cloned.1.call-done = bf16[192,4096]{1,0:T(8,128)(2,1)} async-done(((bf16[192,512]{1,0:T(8,128)(2,1)}), bf16[192,4096]{1,0:T(8,128)(2,1)}) %all-gather.5.cloned.1.call-update) | async-done | bytes 1572880 | tf_op jit(solution)/shard_map/all_gather | solution.py:29
  119.1 9.2 %fusion.98 = f32[192,1792]{1,0:T(8,128)S(1)} fusion(bf16[192,4096]{1,0:T(8,128)(2,1)} %all-gather.5.cloned.1.call-done, bf16[1792,4096]{1,0:T(8,128)(2,1)} %param.11), kind=kOutput, calls=%fused_computation.125 | convolution fusion | flops 2818572288 | bytes 17629184 | tf_op jit(solution)/shard_map/dot_general | solution.py:45
  136.6 10.2 %collective-permute-done = bf16[2,192,1024]{2,1,0:T(8,128)(2,1)S(1)} collective-permute-done((bf16[2,192,1024]{2,1,0:T(8,128)(2,1)S(1)}, bf16[2,192,1024]{2,1,0:T(8,128)(2,1)S(1)}, u32[]{:S(2)}, u32[]{:S(2)}) %collective-permute-start) | collective-permute-done | bytes 786464 | tf_op jit(solution)/shard_map/ppermute | solution.py:22
  146.8 3.4 %convert_add_fusion.1 = f32[2,2,192,896]{3,2,0,1:T(8,128)S(1)} fusion(bf16[2,2,192,896]{3,2,0,1:T(8,128)(2,1)} %collective-permute-done.7, bf16[1024,1792]{1,0:T(8,128)(2,1)S(1)} %copy-done.2, bf16[2,1,192,1024]{3,2,1,0:T(8,128)(2,1)S(1)} %bitcast.251, bf16[2,1,192,1024]{3,2,1,0:T(8,128)(2,1)S(1)} %get-tuple-element.14), kind=kOutput, calls=%fused_computation.14 | convolution fusion | flops 1411448832 | bytes 7536640 | tf_op jit(solution)/shard_map/dot_general | solution.py:56
  157.0 1.8 convert_add_fusion.2
  159.2 6.7 %collective-permute-done.8 = bf16[2,192,896]{2,1,0:T(8,128)(2,1)S(1)} collective-permute-done((bf16[2,192,896]{2,1,0:T(8,128)(2,1)S(1)}, bf16[2,192,896]{2,1,0:T(8,128)(2,1)S(1)}, u32[]{:S(2)}, u32[]{:S(2)}) %collective-permute-start.8) | collective-permute-done | bytes 688160 | tf_op jit(solution)/shard_map/ppermute | solution.py:22
  166.0 14.6 %collective-permute-done.4 = bf16[2,192,896]{2,1,0:T(8,128)(2,1)S(1)} collective-permute-done((bf16[2,192,896]{2,1,0:T(8,128)(2,1)S(1)}, bf16[2,192,896]{2,1,0:T(8,128)(2,1)S(1)}, u32[]{:S(2)}, u32[]{:S(2)}) %collective-permute-start.4) | collective-permute-done | bytes 688160 | tf_op jit(solution)/shard_map/ppermute | solution.py:22
  180.7 14.6 %collective-permute-done.10 = bf16[2,192,896]{2,1,0:T(8,128)(2,1)S(1)} collective-permute-done((bf16[2,192,896]{2,1,0:T(8,128)(2,1)S(1)}, bf16[2,192,896]{2,1,0:T(8,128)(2,1)S(1)}, u32[]{:S(2)}, u32[]{:S(2)}) %collective-permute-start.10) | collective-permute-done | bytes 688160 | tf_op jit(solution)/shard_map/ppermute | solution.py:22
  195.5 14.6 %collective-permute-done.6 = bf16[2,192,896]{2,1,0:T(8,128)(2,1)S(1)} collective-permute-done((bf16[2,192,896]{2,1,0:T(8,128)(2,1)S(1)}, bf16[2,192,896]{2,1,0:T(8,128)(2,1)S(1)}, u32[]{:S(2)}, u32[]{:S(2)}) %collective-permute-start.6) | collective-permute-done | bytes 688160 | tf_op jit(solution)/shard_map/ppermute | solution.py:22
  210.3 10.3 %multiply_reduce_fusion = (f32[192]{0:T(256)S(1)}, f32[192]{0:T(256)S(1)}, bf16[192,896]{1,0:T(8,128)(2,1)S(1)}, bf16[192,896]{1,0:T(8,128)(2,1)S(1)}) fusion(f32[2,192,896]{2,1,0:T(8,128)S(1)} %fusion.64, f32[2,192,896]{2,1,0:T(8,128)S(1)} %fusion.65, f32[192,1792]{1,0:T(8,128)S(1)} %fusion.98, f32[2,192,896]{2,1,0:T(8,128)S(1)} %fusion.66, ...), kind=kLoop, calls=%fused_computation.110 | loop fusion | flops 7396992 | bytes 7570944 | tf_op jit(solution)/shard_map/reduce_sum | solution.py:74
  223.6 2.9 collective-permute-start.18
  226.5 24.7 %collective-permute-done.17 = bf16[4,192,896]{2,1,0:T(8,128)(2,1)S(1)} collective-permute-done((bf16[4,192,896]{2,1,0:T(8,128)(2,1)S(1)}, bf16[4,192,896]{2,1,0:T(8,128)(2,1)S(1)}, u32[]{:S(2)}, u32[]{:S(2)}) %collective-permute-start.17) | collective-permute-done | bytes 1376288 | tf_op jit(solution)/shard_map/ppermute | solution.py:22
  251.2 6.0 %collective-permute-start.19 = (bf16[4,192,896]{2,1,0:T(8,128)(2,1)S(1)}, bf16[4,192,896]{2,1,0:T(8,128)(2,1)S(1)}, u32[]{:S(2)}, u32[]{:S(2)}) collective-permute-start(bf16[4,192,896]{2,1,0:T(8,128)(2,1)S(1)} %collective-permute-done.17), channel_id=1, source_target_pairs={{8,0},{0,8},{24,16},{16,24},{9,1},{1,9},{25,17},{17,25},{10,2},{2,... | collective-permute-start | bytes 4128776 | tf_op jit(solution)/shard_map/ppermute | solution.py:22
  257.3 2.7 collective-permute-done.11
  260.0 2.7 collective-permute-done.12
  262.7 3.3 collective-permute-done.13
  266.1 3.9 %collective-permute-start.16 = (f32[192]{0:T(256)S(1)}, f32[192]{0:T(256)S(1)}, u32[]{:S(2)}, u32[]{:S(2)}) collective-permute-start(f32[192]{0:T(256)S(1)} %add.133), channel_id=1, source_target_pairs={{24,0},{16,8},{8,16},{0,24},{25,1},{17,9},{9,17},{1,25},{26,2},{18... | collective-permute-start | bytes 2312 | tf_op jit(solution)/shard_map/ppermute | solution.py:22
  270.0 13.6 %collective-permute-done.16 = f32[192]{0:T(256)S(1)} collective-permute-done((f32[192]{0:T(256)S(1)}, f32[192]{0:T(256)S(1)}, u32[]{:S(2)}, u32[]{:S(2)}) %collective-permute-start.16) | collective-permute-done | bytes 800 | tf_op jit(solution)/shard_map/ppermute | solution.py:22
  287.9 2.0 collective-permute-done.22
  290.8 2.0 fusion.97
  292.8 3.4 %fusion.14 = f32[1024,896]{0,1:T(8,128)S(1)} fusion(bf16[2,4,192,896]{3,2,0,1:T(8,128)(2,1)S(1)} %get-tuple-element.8, bf16[2,1,192,1024]{3,2,1,0:T(8,128)(2,1)S(1)} %bitcast.240, bf16[2,1,192,1024]{3,2,1,0:T(8,128)(2,1)S(1)} %bitcast.248, bf16[2,1,192,1024]{3,2,1,0:T(8,128)(2,1)S(1)} %bitcast.255, bf16[2,1,192,1024]{3,2,1,0:T(8,128)(2,1)S(1)} %get-tuple-element.14, ...), kind=kOutput, calls=%fused_computation.19 | convolution fusion | flops 2828009472 | bytes 9571328 | tf_op jit(solution)/shard_map/dot_general | solution.py:106
  296.3 4.5 %fusion.17 = f32[1024,896]{0,1:T(8,128)S(1)} fusion(bf16[2,4,192,896]{3,2,0,1:T(8,128)(2,1)S(1)} %get-tuple-element.10, bf16[2,1,192,1024]{3,2,1,0:T(8,128)(2,1)S(1)} %bitcast.241, bf16[2,1,192,1024]{3,2,1,0:T(8,128)(2,1)S(1)} %bitcast.249, bf16[2,1,192,1024]{3,2,1,0:T(8,128)(2,1)} %bitcast.256, bf16[2,1,192,1024]{3,2,1,0:T(8,128)(2,1)S(1)} %get-tuple-element.14, ...), kind=kOutput, calls=%fused_computation.20 | convolution fusion | flops 2828009472 | bytes 9571328 | tf_op jit(solution)/shard_map/dot_general | solution.py:106
  300.8 3.8 %pad_maximum_fusion.1 = f32[1024,1792]{0,1:T(8,128)} fusion(f32[1024,896]{0,1:T(8,128)S(1)} %fusion.17, f32[1024,896]{0,1:T(8,128)S(1)} %fusion.14), kind=kLoop, calls=%fused_computation.1 | loop fusion | flops 1835008 | bytes 14680064 | tf_op jit(solution)/shard_map/concatenate | solution.py:110
  304.6 8.4 %copy.25 = f32[1024,1792]{1,0:T(8,128)} copy(f32[1024,1792]{0,1:T(8,128)} %pad_maximum_fusion.1) | data formatting | bytes 14680064
  312.9 6.0 %fusion.11 = f32[1024,896]{0,1:T(8,128)S(1)} fusion(bf16[2,4,192,896]{3,2,0,1:T(8,128)(2,1)} %get-tuple-element.11, bf16[2,1,192,1024]{3,2,1,0:T(8,128)(2,1)} %bitcast.236, bf16[2,1,192,1024]{3,2,1,0:T(8,128)(2,1)} %bitcast.244, bf16[2,1,192,1024]{3,2,1,0:T(8,128)(2,1)} %bitcast.257, bf16[2,1,192,1024]{3,2,1,0:T(8,128)(2,1)S(1)} %get-tuple-element.14, ...), kind=kOutput, calls=%fused_computation.18 | convolution fusion | flops 2828009472 | bytes 9571328 | tf_op jit(solution)/shard_map/dot_general | solution.py:106
  319.0 3.4 fusion.8
  322.4 3.6 %pad_maximum_fusion = f32[1024,1792]{0,1:T(8,128)} fusion(f32[1024,896]{0,1:T(8,128)S(1)} %fusion.11, f32[1024,896]{0,1:T(8,128)S(1)} %fusion.8), kind=kLoop, calls=%fused_computation | loop fusion | flops 1835008 | bytes 14680064 | tf_op jit(solution)/shard_map/concatenate | solution.py:110
  326.0 8.4 %copy.24 = f32[1024,1792]{1,0:T(8,128)} copy(f32[1024,1792]{0,1:T(8,128)} %pad_maximum_fusion) | data formatting | bytes 14680064
  (90 shorter events, 28.9 us)
Async XLA Ops:
  7.2 67.4 %all-gather.3.cloned.1.call-start = ((), (), s32[]{:S(2)}) async-start(), calls=%async_computation | async-start | bytes 3538944 | tf_op jit(solution)/shard_map/all_gather | solution.py:28
  9.0 110.1 %all-gather.5.cloned.1.call-start = ((), (), s32[]{:S(2)}) async-start(), calls=%async_computation.1 | async-start | bytes 1769472 | tf_op jit(solution)/shard_map/all_gather | solution.py:29
  74.6 22.5 %copy-start.1 = (bf16[1024,1792]{1,0:T(8,128)(2,1)S(1)}, bf16[1024,1792]{1,0:T(8,128)(2,1)}, u32[]{:S(2)}) copy-start(bf16[1024,1792]{1,0:T(8,128)(2,1)} %param.9) | copy-start | bytes 11010052
  77.1 20.0 %collective-permute-start.2 = (bf16[2,192,1024]{2,1,0:T(8,128)(2,1)S(1)}, bf16[2,192,1024]{2,1,0:T(8,128)(2,1)S(1)}, u32[]{:S(2)}, u32[]{:S(2)}) collective-permute-start(bf16[2,192,1024]{2,1,0:T(8,128)(2,1)S(1)} %get-tuple-element.15), channel_id=1, source_target_pairs={{24,0},{16,8},{8,16},{0,24},{25,1},{17,9},{9,17},{1,25},{26,2},{18... | collective-permute-start | bytes 2359304 | tf_op jit(solution)/shard_map/ppermute | solution.py:22
  78.8 18.3 %collective-permute-start.1 = (bf16[2,192,1024]{2,1,0:T(8,128)(2,1)S(1)}, bf16[2,192,1024]{2,1,0:T(8,128)(2,1)S(1)}, u32[]{:S(2)}, u32[]{:S(2)}) collective-permute-start(bf16[2,192,1024]{2,1,0:T(8,128)(2,1)S(1)} %get-tuple-element.16), channel_id=1, source_target_pairs={{8,0},{0,8},{24,16},{16,24},{9,1},{1,9},{25,17},{17,25},{10,2},{2,... | collective-permute-start | bytes 2359304 | tf_op jit(solution)/shard_map/ppermute | solution.py:22
  100.0 46.8 %collective-permute-start.7 = (bf16[2,2,192,896]{3,2,0,1:T(8,128)(2,1)}, bf16[2,2,192,896]{3,2,0,1:T(8,128)(2,1)}, u32[]{:S(2)}, u32[]{:S(2)}) collective-permute-start(bf16[2,2,192,896]{3,2,0,1:T(8,128)(2,1)} %fusion.50), channel_id=1, source_target_pairs={{8,0},{0,8},{24,16},{16,24},{9,1},{1,9},{25,17},{17,25},{10,2},{2,... | collective-permute-start | bytes 4128776 | tf_op jit(solution)/shard_map/ppermute | solution.py:22
  100.3 29.2 %copy-start.5 = (bf16[2,192,1024]{2,1,0:T(8,128)(2,1)S(1)}, bf16[2,192,1024]{2,1,0:T(8,128)(2,1)}, u32[]{:S(2)}) copy-start(bf16[2,192,1024]{2,1,0:T(8,128)(2,1)} %copy-done.4) | copy-start | bytes 2359300
  100.4 29.2 %copy-start.9 = (bf16[2,192,1024]{2,1,0:T(8,128)(2,1)S(1)}, bf16[2,192,1024]{2,1,0:T(8,128)(2,1)}, u32[]{:S(2)}) copy-start(bf16[2,192,1024]{2,1,0:T(8,128)(2,1)} %copy-done.8) | copy-start | bytes 2359300
  119.1 10.4 %copy-start.2 = (bf16[1024,1792]{1,0:T(8,128)(2,1)S(1)}, bf16[1024,1792]{1,0:T(8,128)(2,1)}, u32[]{:S(2)}) copy-start(bf16[1024,1792]{1,0:T(8,128)(2,1)} %param.9) | copy-start | bytes 11010052
  128.3 18.5 %collective-permute-start = (bf16[2,192,1024]{2,1,0:T(8,128)(2,1)S(1)}, bf16[2,192,1024]{2,1,0:T(8,128)(2,1)S(1)}, u32[]{:S(2)}, u32[]{:S(2)}) collective-permute-start(bf16[2,192,1024]{2,1,0:T(8,128)(2,1)S(1)} %get-tuple-element.17), channel_id=1, source_target_pairs={{16,0},{24,8},{0,16},{8,24},{17,1},{25,9},{1,17},{9,25},{18,2},{26... | collective-permute-start | bytes 2359304 | tf_op jit(solution)/shard_map/ppermute | solution.py:22
  131.4 20.2 %collective-permute-start.3 = (bf16[2,2,192,896]{3,2,1,0:T(8,128)(2,1)S(1)}, bf16[2,2,192,896]{3,2,1,0:T(8,128)(2,1)S(1)}, u32[]{:S(2)}, u32[]{:S(2)}) collective-permute-start(bf16[2,2,192,896]{3,2,1,0:T(8,128)(2,1)S(1)} %fusion.44), channel_id=1, source_target_pairs={{8,0},{0,8},{24,16},{16,24},{9,1},{1,9},{25,17},{17,25},{10,2},{2,... | collective-permute-start | bytes 4128776 | tf_op jit(solution)/shard_map/ppermute | solution.py:22
  134.2 19.7 %collective-permute-start.9 = (bf16[2,2,192,896]{3,2,0,1:T(8,128)(2,1)S(1)}, bf16[2,2,192,896]{3,2,0,1:T(8,128)(2,1)S(1)}, u32[]{:S(2)}, u32[]{:S(2)}) collective-permute-start(bf16[2,2,192,896]{3,2,0,1:T(8,128)(2,1)S(1)} %fusion.53), channel_id=1, source_target_pairs={{8,0},{0,8},{24,16},{16,24},{9,1},{1,9},{25,17},{17,25},{10,2},{2,... | collective-permute-start | bytes 4128776 | tf_op jit(solution)/shard_map/ppermute | solution.py:22
  136.0 20.9 %collective-permute-start.5 = (bf16[2,2,192,896]{3,2,0,1:T(8,128)(2,1)S(1)}, bf16[2,2,192,896]{3,2,0,1:T(8,128)(2,1)S(1)}, u32[]{:S(2)}, u32[]{:S(2)}) collective-permute-start(bf16[2,2,192,896]{3,2,0,1:T(8,128)(2,1)S(1)} %fusion.47), channel_id=1, source_target_pairs={{8,0},{0,8},{24,16},{16,24},{9,1},{1,9},{25,17},{17,25},{10,2},{2,... | collective-permute-start | bytes 4128776 | tf_op jit(solution)/shard_map/ppermute | solution.py:22
  146.8 146.0 %copy-start.13 = (bf16[2,192,1024]{2,1,0:T(8,128)(2,1)}, bf16[2,192,1024]{2,1,0:T(8,128)(2,1)S(1)}, u32[]{:S(2)}) copy-start(bf16[2,192,1024]{2,1,0:T(8,128)(2,1)S(1)} %collective-permute-done) | copy-start | bytes 2359300
  150.3 15.6 %collective-permute-start.8 = (bf16[2,192,896]{2,1,0:T(8,128)(2,1)S(1)}, bf16[2,192,896]{2,1,0:T(8,128)(2,1)S(1)}, u32[]{:S(2)}, u32[]{:S(2)}) collective-permute-start(bf16[2,192,896]{2,1,0:T(8,128)(2,1)S(1)} %fusion.92), channel_id=1, source_target_pairs={{16,0},{24,8},{0,16},{8,24},{17,1},{25,9},{1,17},{9,25},{18,2},{26... | collective-permute-start | bytes 2064392 | tf_op jit(solution)/shard_map/ppermute | solution.py:22
  153.5 27.1 %collective-permute-start.4 = (bf16[2,192,896]{2,1,0:T(8,128)(2,1)S(1)}, bf16[2,192,896]{2,1,0:T(8,128)(2,1)S(1)}, u32[]{:S(2)}, u32[]{:S(2)}) collective-permute-start(bf16[2,192,896]{2,1,0:T(8,128)(2,1)S(1)} %fusion.90), channel_id=1, source_target_pairs={{16,0},{24,8},{0,16},{8,24},{17,1},{25,9},{1,17},{9,25},{18,2},{26... | collective-permute-start | bytes 2064392 | tf_op jit(solution)/shard_map/ppermute | solution.py:22
  155.7 39.7 %collective-permute-start.10 = (bf16[2,192,896]{2,1,0:T(8,128)(2,1)S(1)}, bf16[2,192,896]{2,1,0:T(8,128)(2,1)S(1)}, u32[]{:S(2)}, u32[]{:S(2)}) collective-permute-start(bf16[2,192,896]{2,1,0:T(8,128)(2,1)S(1)} %fusion.93), channel_id=1, source_target_pairs={{16,0},{24,8},{0,16},{8,24},{17,1},{25,9},{1,17},{9,25},{18,2},{26... | collective-permute-start | bytes 2064392 | tf_op jit(solution)/shard_map/ppermute | solution.py:22
  158.9 51.3 %collective-permute-start.6 = (bf16[2,192,896]{2,1,0:T(8,128)(2,1)S(1)}, bf16[2,192,896]{2,1,0:T(8,128)(2,1)S(1)}, u32[]{:S(2)}, u32[]{:S(2)}) collective-permute-start(bf16[2,192,896]{2,1,0:T(8,128)(2,1)S(1)} %fusion.91), channel_id=1, source_target_pairs={{16,0},{24,8},{0,16},{8,24},{17,1},{25,9},{1,17},{9,25},{18,2},{26... | collective-permute-start | bytes 2064392 | tf_op jit(solution)/shard_map/ppermute | solution.py:22
  221.8 29.4 %collective-permute-start.17 = (bf16[4,192,896]{2,1,0:T(8,128)(2,1)S(1)}, bf16[4,192,896]{2,1,0:T(8,128)(2,1)S(1)}, u32[]{:S(2)}, u32[]{:S(2)}) collective-permute-start(bf16[4,192,896]{2,1,0:T(8,128)(2,1)S(1)} %pad_maximum_fusion.6), channel_id=1, source_target_pairs={{16,0},{24,8},{0,16},{8,24},{17,1},{25,9},{1,17},{9,25},{18,2},{26... | collective-permute-start | bytes 4128776 | tf_op jit(solution)/shard_map/ppermute | solution.py:22
  223.3 61.5 %collective-permute-start.20 = (bf16[4,192,896]{2,1,0:T(8,128)(2,1)S(1)}, bf16[4,192,896]{2,1,0:T(8,128)(2,1)S(1)}, u32[]{:S(2)}, u32[]{:S(2)}) collective-permute-start(bf16[4,192,896]{2,1,0:T(8,128)(2,1)S(1)} %pad_maximum_fusion.7), channel_id=1, source_target_pairs={{16,0},{24,8},{0,16},{8,24},{17,1},{25,9},{1,17},{9,25},{18,2},{26... | collective-permute-start | bytes 4128776 | tf_op jit(solution)/shard_map/ppermute | solution.py:22
  223.6 62.6 %collective-permute-start.18 = (bf16[4,192,896]{2,1,0:T(8,128)(2,1)S(1)}, bf16[4,192,896]{2,1,0:T(8,128)(2,1)S(1)}, u32[]{:S(2)}, u32[]{:S(2)}) collective-permute-start(bf16[4,192,896]{2,1,0:T(8,128)(2,1)S(1)} %pad_maximum_fusion.6), channel_id=1, source_target_pairs={{8,0},{0,8},{24,16},{16,24},{9,1},{1,9},{25,17},{17,25},{10,2},{2,... | collective-permute-start | bytes 4128776 | tf_op jit(solution)/shard_map/ppermute | solution.py:22
  251.2 34.9 %collective-permute-start.19 = (bf16[4,192,896]{2,1,0:T(8,128)(2,1)S(1)}, bf16[4,192,896]{2,1,0:T(8,128)(2,1)S(1)}, u32[]{:S(2)}, u32[]{:S(2)}) collective-permute-start(bf16[4,192,896]{2,1,0:T(8,128)(2,1)S(1)} %collective-permute-done.17), channel_id=1, source_target_pairs={{8,0},{0,8},{24,16},{16,24},{9,1},{1,9},{25,17},{17,25},{10,2},{2,... | collective-permute-start | bytes 4128776 | tf_op jit(solution)/shard_map/ppermute | solution.py:22
  257.3 2.7 collective-permute-start.11
  260.0 2.7 collective-permute-start.12
  262.7 3.3 collective-permute-start.13
  266.1 21.1 %copy-start = (f32[192]{0:T(256)}, f32[192]{0:T(256)S(1)}, u32[]{:S(2)}) copy-start(f32[192]{0:T(256)S(1)} %add.133) | copy-start | bytes 2308
  266.1 17.5 %collective-permute-start.16 = (f32[192]{0:T(256)S(1)}, f32[192]{0:T(256)S(1)}, u32[]{:S(2)}, u32[]{:S(2)}) collective-permute-start(f32[192]{0:T(256)S(1)} %add.133), channel_id=1, source_target_pairs={{24,0},{16,8},{8,16},{0,24},{25,1},{17,9},{9,17},{1,25},{26,2},{18... | collective-permute-start | bytes 2312 | tf_op jit(solution)/shard_map/ppermute | solution.py:22
  270.0 14.8 %collective-permute-start.15 = (f32[192]{0:T(256)S(1)}, f32[192]{0:T(256)S(1)}, u32[]{:S(2)}, u32[]{:S(2)}) collective-permute-start(f32[192]{0:T(256)S(1)} %add.133), channel_id=1, source_target_pairs={{8,0},{0,8},{24,16},{16,24},{9,1},{1,9},{25,17},{17,25},{10,2},{2,... | collective-permute-start | bytes 2312 | tf_op jit(solution)/shard_map/ppermute | solution.py:22
  283.6 2.6 collective-permute-start.14
  284.8 3.1 collective-permute-start.21
  284.8 5.1 %collective-permute-start.22 = (bf16[4,192,896]{2,1,0:T(8,128)(2,1)S(1)}, bf16[4,192,896]{2,1,0:T(8,128)(2,1)S(1)}, u32[]{:S(2)}, u32[]{:S(2)}) collective-permute-start(bf16[4,192,896]{2,1,0:T(8,128)(2,1)S(1)} %collective-permute-done.20), channel_id=1, source_target_pairs={{8,0},{0,8},{24,16},{16,24},{9,1},{1,9},{25,17},{17,25},{10,2},{2,... | collective-permute-start | bytes 4128776 | tf_op jit(solution)/shard_map/ppermute | solution.py:22
  312.9 6.0 %copy-start.14 = (bf16[2,192,1024]{2,1,0:T(8,128)(2,1)S(1)}, bf16[2,192,1024]{2,1,0:T(8,128)(2,1)}, u32[]{:S(2)}) copy-start(bf16[2,192,1024]{2,1,0:T(8,128)(2,1)} %copy-done.13) | copy-start | bytes 2359300
  (8 other events, 31.2 us)
Sparse Core Ops, SparseCore 0:
  10.6 63.9 all-gather.2
  76.6 42.4 all-gather.4
where the time goes:
time: 345 us; the launch traced here: 341 us
  waiting for transfers between devices  213 us (62%)
  matrix products  43.6 us (13%)
  starting transfers between devices  24.5 us (7%)
  other arithmetic  23.3 us (7%)
  local copies, waits for them, and re-layouts  22.1 us (6%)
  between operations  14.6 us (4%)
    ppermute x20, waiting for transfers between devices, shift(): return lax.ppermute(value, 'dp', pairs)  120 us
    all_gather x1, waiting for transfers between devices, body(): full = lax.all_gather(both, 'tensor', axis=2, tiled=True)  64.7 us
    ppermute x20, starting transfers between devices, shift(): return lax.ppermute(value, 'dp', pairs)  24.4 us
    all_gather x1, waiting for transfers between devices, body(): full_probe = lax.all_gather(probes, 'tensor', axis=1, tiled=True)  18.7 us
    dot_general x4, matrix products, body(): lax.dot_general(scaled, flat[at], (((0,), (0,)), ((), ())), preferred_ele...  17.4 us
    dot_general x8, matrix products, partial(): jnp.dot(left, weight, preferred_element_type=f32)  17.1 us
    unnamed x32, local copies, waits for them, and re-layouts  16.8 us
    reduce_sum x1, other arithmetic, body(): projection = projection + jnp.sum(hidden_dot * out, axis=1)  10.3 us
  transfers between devices with their start and end apart: 25, of which 16 were waited for; matrix products, arithmetic and copies ran while one was open for 9% of the time, Pallas kernels for 0%

commit v1 on v0

--- a/solution.py
+++ b/solution.py
@@ -25,7 +25,14 @@
         return (me // CORES + step) % chips * CORES + (me % CORES ^ flip)
 
     both = jnp.stack([tokens, tangents], axis=0)
-    full = lax.all_gather(both, "tensor", axis=2, tiled=True)
+    ring = [both]
+    for hop in range(7):
+        ring.append(lax.ppermute(ring[-1], "tensor", [(dev, (dev + 1) % 8) for dev in range(8)]))
+    full = jnp.roll(
+        jnp.concatenate(ring[::-1], axis=2),
+        (lax.axis_index("tensor") + 1) * ring[0].shape[2],
+        axis=2,
+    )
     full_probe = lax.all_gather(probes, "tensor", axis=1, tiled=True)
 
     def columns(at):

time: 345 us -> 339 us (0.983)
  the two profiles are of different devices: /device:TPU:5 before, /device:TPU:0 now
where the time goes in v1:
time: 339 us; the launch traced here: 333 us
  waiting for transfers between devices  212 us (63%)
  matrix products  50.2 us (15%)
  local copies, waits for them, and re-layouts  22.3 us (7%)
  starting transfers between devices  19.7 us (6%)
  between operations  14.9 us (4%)
  other arithmetic  14.1 us (4%)
    ppermute x20, waiting for transfers between devices, shift(): return lax.ppermute(value, 'dp', pairs)  114 us
    ppermute x7, waiting for transfers between devices, body(): lax.ppermute(ring[-1], 'tensor', [(dev, (dev + 1) % 8) for dev in range(8)])  80.1 us
    dot_general x8, matrix products, partial(): jnp.dot(left, weight, preferred_element_type=f32)  21.3 us
    dot_general x4, matrix products, body(): lax.dot_general(scaled, flat[at], (((0,), (0,)), ((), ())), preferred_ele...  19.6 us
    unnamed x44, local copies, waits for them, and re-layouts  17.6 us
    ppermute x20, starting transfers between devices, shift(): return lax.ppermute(value, 'dp', pairs)  13.3 us
    all_gather x1, waiting for transfers between devices, body(): full_probe = lax.all_gather(probes, 'tensor', axis=1, tiled=True)  9.65 us
    dot_general x1, matrix products, body(): lax.dot_general(full_probe, w_down, (((1,), (1,)), ((), ())), preferred_e...  9.25 us
  transfers between devices with their start and end apart: 31, of which 20 were waited for; matrix products, arithmetic and copies ran while one was open for 11% of the time, Pallas kernels for 0%

profile of v1, /device:TPU:0, one launch (start us, length us, event | category | flops | bytes accessed | tf_op | source)
XLA Modules:
  0.0 333.0 jit_solution(8094953568665512361)
XLA Ops:
  8.3 3.0 collective-permute-start
  11.3 12.2 %collective-permute-done = bf16[2,192,512]{2,1,0:T(8,128)(2,1)S(1)} collective-permute-done((bf16[2,192,512]{2,1,0:T(8,128)(2,1)S(1)}, bf16[2,192,512]{2,1,0:T(8,128)(2,1)S(1)}, u32[]{:S(2)}, u32[]{:S(2)}) %collective-permute-start) | collective-permute-done | bytes 393248 | tf_op jit(solution)/shard_map/ppermute | solution.py:30
  23.5 13.0 %collective-permute-done.1 = bf16[2,192,512]{2,1,0:T(8,128)(2,1)S(1)} collective-permute-done((bf16[2,192,512]{2,1,0:T(8,128)(2,1)S(1)}, bf16[2,192,512]{2,1,0:T(8,128)(2,1)S(1)}, u32[]{:S(2)}, u32[]{:S(2)}) %collective-permute-start.1) | collective-permute-done | bytes 393248 | tf_op jit(solution)/shard_map/ppermute | solution.py:30
  36.5 12.1 %collective-permute-done.2 = bf16[2,192,512]{2,1,0:T(8,128)(2,1)S(1)} collective-permute-done((bf16[2,192,512]{2,1,0:T(8,128)(2,1)S(1)}, bf16[2,192,512]{2,1,0:T(8,128)(2,1)S(1)}, u32[]{:S(2)}, u32[]{:S(2)}) %collective-permute-start.2) | collective-permute-done | bytes 393248 | tf_op jit(solution)/shard_map/ppermute | solution.py:30
  48.6 11.3 %collective-permute-done.3 = bf16[2,192,512]{2,1,0:T(8,128)(2,1)S(1)} collective-permute-done((bf16[2,192,512]{2,1,0:T(8,128)(2,1)S(1)}, bf16[2,192,512]{2,1,0:T(8,128)(2,1)S(1)}, u32[]{:S(2)}, u32[]{:S(2)}) %collective-permute-start.3) | collective-permute-done | bytes 393248 | tf_op jit(solution)/shard_map/ppermute | solution.py:30
  59.8 10.5 %collective-permute-done.4 = bf16[2,192,512]{2,1,0:T(8,128)(2,1)S(1)} collective-permute-done((bf16[2,192,512]{2,1,0:T(8,128)(2,1)S(1)}, bf16[2,192,512]{2,1,0:T(8,128)(2,1)S(1)}, u32[]{:S(2)}, u32[]{:S(2)}) %collective-permute-start.4) | collective-permute-done | bytes 393248 | tf_op jit(solution)/shard_map/ppermute | solution.py:30
  70.3 10.8 %collective-permute-done.5 = bf16[2,192,512]{2,1,0:T(8,128)(2,1)S(1)} collective-permute-done((bf16[2,192,512]{2,1,0:T(8,128)(2,1)S(1)}, bf16[2,192,512]{2,1,0:T(8,128)(2,1)S(1)}, u32[]{:S(2)}, u32[]{:S(2)}) %collective-permute-start.5) | collective-permute-done | bytes 393248 | tf_op jit(solution)/shard_map/ppermute | solution.py:30
  81.2 10.3 %collective-permute-done.6 = bf16[2,192,512]{2,1,0:T(8,128)(2,1)S(1)} collective-permute-done((bf16[2,192,512]{2,1,0:T(8,128)(2,1)S(1)}, bf16[2,192,512]{2,1,0:T(8,128)(2,1)S(1)}, u32[]{:S(2)}, u32[]{:S(2)}) %collective-permute-start.6) | collective-permute-done | bytes 393248 | tf_op jit(solution)/shard_map/ppermute | solution.py:30
  96.5 17.7 %collective-permute-done.9 = bf16[2,192,1024]{2,1,0:T(8,128)(2,1)S(1)} collective-permute-done((bf16[2,192,1024]{2,1,0:T(8,128)(2,1)S(1)}, bf16[2,192,1024]{2,1,0:T(8,128)(2,1)S(1)}, u32[]{:S(2)}, u32[]{:S(2)}) %collective-permute-start.9) | collective-permute-done | bytes 786464 | tf_op jit(solution)/shard_map/ppermute | solution.py:22
  117.1 9.6 %all-gather.2.cloned.1.call-done = bf16[192,4096]{1,0:T(8,128)(2,1)} async-done(((bf16[192,512]{1,0:T(8,128)(2,1)}), bf16[192,4096]{1,0:T(8,128)(2,1)}) %all-gather.2.cloned.1.call-update) | async-done | bytes 1572880 | tf_op jit(solution)/shard_map/all_gather | solution.py:36
  126.8 9.2 %fusion.98 = f32[192,1792]{1,0:T(8,128)S(1)} fusion(bf16[192,4096]{1,0:T(8,128)(2,1)} %all-gather.2.cloned.1.call-done, bf16[1792,4096]{1,0:T(8,128)(2,1)} %param.11), kind=kOutput, calls=%fused_computation.141 | convolution fusion | flops 2818572288 | bytes 17629184 | tf_op jit(solution)/shard_map/dot_general | solution.py:52
  136.1 3.1 fusion.44
  143.5 3.0 convert_add_fusion.1
  148.1 2.9 convert_add_fusion.3
  151.8 3.0 convert_add_fusion
  156.3 2.9 convert_add_fusion.2
  160.0 4.9 %collective-permute-done.15 = bf16[2,192,896]{2,1,0:T(8,128)(2,1)S(1)} collective-permute-done((bf16[2,192,896]{2,1,0:T(8,128)(2,1)S(1)}, bf16[2,192,896]{2,1,0:T(8,128)(2,1)S(1)}, u32[]{:S(2)}, u32[]{:S(2)}) %collective-permute-start.15) | collective-permute-done | bytes 688160 | tf_op jit(solution)/shard_map/ppermute | solution.py:22
  165.1 14.6 %collective-permute-done.11 = bf16[2,192,896]{2,1,0:T(8,128)(2,1)S(1)} collective-permute-done((bf16[2,192,896]{2,1,0:T(8,128)(2,1)S(1)}, bf16[2,192,896]{2,1,0:T(8,128)(2,1)S(1)}, u32[]{:S(2)}, u32[]{:S(2)}) %collective-permute-start.11) | collective-permute-done | bytes 688160 | tf_op jit(solution)/shard_map/ppermute | solution.py:22
  179.9 14.6 %collective-permute-done.17 = bf16[2,192,896]{2,1,0:T(8,128)(2,1)S(1)} collective-permute-done((bf16[2,192,896]{2,1,0:T(8,128)(2,1)S(1)}, bf16[2,192,896]{2,1,0:T(8,128)(2,1)S(1)}, u32[]{:S(2)}, u32[]{:S(2)}) %collective-permute-start.17) | collective-permute-done | bytes 688160 | tf_op jit(solution)/shard_map/ppermute | solution.py:22
  194.6 14.1 %collective-permute-done.13 = bf16[2,192,896]{2,1,0:T(8,128)(2,1)S(1)} collective-permute-done((bf16[2,192,896]{2,1,0:T(8,128)(2,1)S(1)}, bf16[2,192,896]{2,1,0:T(8,128)(2,1)S(1)}, u32[]{:S(2)}, u32[]{:S(2)}) %collective-permute-start.13) | collective-permute-done | bytes 688160 | tf_op jit(solution)/shard_map/ppermute | solution.py:22
  214.1 30.7 %collective-permute-done.24 = bf16[4,192,896]{2,1,0:T(8,128)(2,1)S(1)} collective-permute-done((bf16[4,192,896]{2,1,0:T(8,128)(2,1)S(1)}, bf16[4,192,896]{2,1,0:T(8,128)(2,1)S(1)}, u32[]{:S(2)}, u32[]{:S(2)}) %collective-permute-start.24) | collective-permute-done | bytes 1376288 | tf_op jit(solution)/shard_map/ppermute | solution.py:22
  248.8 3.3 collective-permute-done.19
  253.6 3.0 collective-permute-done.20
  258.1 13.9 %collective-permute-done.23 = f32[192]{0:T(256)S(1)} collective-permute-done((f32[192]{0:T(256)S(1)}, f32[192]{0:T(256)S(1)}, u32[]{:S(2)}, u32[]{:S(2)}) %collective-permute-start.23) | collective-permute-done | bytes 800 | tf_op jit(solution)/shard_map/ppermute | solution.py:22
  282.0 4.5 %fusion.14 = f32[1024,896]{0,1:T(8,128)S(1)} fusion(bf16[2,4,192,896]{3,2,0,1:T(8,128)(2,1)S(1)} %get-tuple-element.12, bf16[2,1,192,1024]{3,2,1,0:T(8,128)(2,1)S(1)} %bitcast.244, bf16[2,1,192,1024]{3,2,1,0:T(8,128)(2,1)S(1)} %bitcast.252, bf16[2,1,192,1024]{3,2,1,0:T(8,128)(2,1)} %bitcast.3, bf16[2,1,192,1024]{3,2,1,0:T(8,128)(2,1)S(1)} %get-tuple-element.8, ...), kind=kOutput, calls=%fused_computation.19 | convolution fusion | flops 2828009472 | bytes 9571328 | tf_op jit(solution)/shard_map/dot_general | solution.py:113
  286.6 4.5 %fusion.17 = f32[1024,896]{0,1:T(8,128)S(1)} fusion(bf16[2,4,192,896]{3,2,0,1:T(8,128)(2,1)S(1)} %get-tuple-element.14, bf16[2,1,192,1024]{3,2,1,0:T(8,128)(2,1)S(1)} %bitcast.245, bf16[2,1,192,1024]{3,2,1,0:T(8,128)(2,1)S(1)} %bitcast.253, bf16[2,1,192,1024]{3,2,1,0:T(8,128)(2,1)} %bitcast.3, bf16[2,1,192,1024]{3,2,1,0:T(8,128)(2,1)S(1)} %get-tuple-element.8, ...), kind=kOutput, calls=%fused_computation.20 | convolution fusion | flops 2828009472 | bytes 9571328 | tf_op jit(solution)/shard_map/dot_general | solution.py:113
  291.1 3.8 %pad_maximum_fusion.1 = f32[1024,1792]{0,1:T(8,128)} fusion(f32[1024,896]{0,1:T(8,128)S(1)} %fusion.17, f32[1024,896]{0,1:T(8,128)S(1)} %fusion.14), kind=kLoop, calls=%fused_computation.1 | loop fusion | flops 1835008 | bytes 14680064 | tf_op jit(solution)/shard_map/concatenate | solution.py:117
  294.9 8.6 %copy.25 = f32[1024,1792]{1,0:T(8,128)} copy(f32[1024,1792]{0,1:T(8,128)} %pad_maximum_fusion.1) | data formatting | bytes 14680064
  303.4 6.0 %fusion.11 = f32[1024,896]{0,1:T(8,128)S(1)} fusion(bf16[2,4,192,896]{3,2,0,1:T(8,128)(2,1)} %get-tuple-element.15, bf16[2,1,192,1024]{3,2,1,0:T(8,128)(2,1)} %bitcast.240, bf16[2,1,192,1024]{3,2,1,0:T(8,128)(2,1)} %bitcast.249, bf16[2,1,192,1024]{3,2,1,0:T(8,128)(2,1)} %bitcast.3, bf16[2,1,192,1024]{3,2,1,0:T(8,128)(2,1)S(1)} %get-tuple-element.8, ...), kind=kOutput, calls=%fused_computation.18 | convolution fusion | flops 2828009472 | bytes 9571328 | tf_op jit(solution)/shard_map/dot_general | solution.py:113
  309.4 4.5 %fusion.8 = f32[1024,896]{0,1:T(8,128)S(1)} fusion(bf16[2,4,192,896]{3,2,0,1:T(8,128)(2,1)S(1)} %get-tuple-element.13, bf16[2,1,192,1024]{3,2,1,0:T(8,128)(2,1)S(1)} %bitcast.246, bf16[2,1,192,1024]{3,2,1,0:T(8,128)(2,1)S(1)} %bitcast.254, bf16[2,1,192,1024]{3,2,1,0:T(8,128)(2,1)} %bitcast.3, bf16[2,1,192,1024]{3,2,1,0:T(8,128)(2,1)S(1)} %get-tuple-element.8, ...), kind=kOutput, calls=%fused_computation.17 | convolution fusion | flops 2828009472 | bytes 9571328 | tf_op jit(solution)/shard_map/dot_general | solution.py:113
  314.0 3.6 %pad_maximum_fusion = f32[1024,1792]{0,1:T(8,128)} fusion(f32[1024,896]{0,1:T(8,128)S(1)} %fusion.11, f32[1024,896]{0,1:T(8,128)S(1)} %fusion.8), kind=kLoop, calls=%fused_computation | loop fusion | flops 1835008 | bytes 14680064 | tf_op jit(solution)/shard_map/concatenate | solution.py:117
  317.6 8.4 %copy.24 = f32[1024,1792]{1,0:T(8,128)} copy(f32[1024,1792]{0,1:T(8,128)} %pad_maximum_fusion) | data formatting | bytes 14680064
  (115 shorter events, 40.5 us)
Async XLA Ops:
  7.2 119.6 %all-gather.2.cloned.1.call-start = ((), (), s32[]{:S(2)}) async-start(), calls=%async_computation | async-start | bytes 1769472 | tf_op jit(solution)/shard_map/all_gather | solution.py:36
  8.3 15.2 %collective-permute-start = (bf16[2,192,512]{2,1,0:T(8,128)(2,1)S(1)}, bf16[2,192,512]{2,1,0:T(8,128)(2,1)S(1)}, u32[]{:S(2)}, u32[]{:S(2)}) collective-permute-start(bf16[2,192,512]{2,1,0:T(8,128)(2,1)S(1)} %pad_maximum_fusion.8), channel_id=1, source_target_pairs={{0,1},{1,2},{2,3},{3,4},{4,5},{5,6},{6,7},{7,0},{8,9},{9,10},{10,1... | collective-permute-start | bytes 1179656 | tf_op jit(solution)/shard_map/ppermute | solution.py:30
  23.5 13.0 %collective-permute-start.1 = (bf16[2,192,512]{2,1,0:T(8,128)(2,1)S(1)}, bf16[2,192,512]{2,1,0:T(8,128)(2,1)S(1)}, u32[]{:S(2)}, u32[]{:S(2)}) collective-permute-start(bf16[2,192,512]{2,1,0:T(8,128)(2,1)S(1)} %collective-permute-done), channel_id=1, source_target_pairs={{0,1},{1,2},{2,3},{3,4},{4,5},{5,6},{6,7},{7,0},{8,9},{9,10},{10,1... | collective-permute-start | bytes 1179656 | tf_op jit(solution)/shard_map/ppermute | solution.py:30
  36.5 12.1 %collective-permute-start.2 = (bf16[2,192,512]{2,1,0:T(8,128)(2,1)S(1)}, bf16[2,192,512]{2,1,0:T(8,128)(2,1)S(1)}, u32[]{:S(2)}, u32[]{:S(2)}) collective-permute-start(bf16[2,192,512]{2,1,0:T(8,128)(2,1)S(1)} %collective-permute-done.1), channel_id=1, source_target_pairs={{0,1},{1,2},{2,3},{3,4},{4,5},{5,6},{6,7},{7,0},{8,9},{9,10},{10,1... | collective-permute-start | bytes 1179656 | tf_op jit(solution)/shard_map/ppermute | solution.py:30
  48.6 11.3 %collective-permute-start.3 = (bf16[2,192,512]{2,1,0:T(8,128)(2,1)S(1)}, bf16[2,192,512]{2,1,0:T(8,128)(2,1)S(1)}, u32[]{:S(2)}, u32[]{:S(2)}) collective-permute-start(bf16[2,192,512]{2,1,0:T(8,128)(2,1)S(1)} %collective-permute-done.2), channel_id=1, source_target_pairs={{0,1},{1,2},{2,3},{3,4},{4,5},{5,6},{6,7},{7,0},{8,9},{9,10},{10,1... | collective-permute-start | bytes 1179656 | tf_op jit(solution)/shard_map/ppermute | solution.py:30
  59.8 10.5 %collective-permute-start.4 = (bf16[2,192,512]{2,1,0:T(8,128)(2,1)S(1)}, bf16[2,192,512]{2,1,0:T(8,128)(2,1)S(1)}, u32[]{:S(2)}, u32[]{:S(2)}) collective-permute-start(bf16[2,192,512]{2,1,0:T(8,128)(2,1)S(1)} %collective-permute-done.3), channel_id=1, source_target_pairs={{0,1},{1,2},{2,3},{3,4},{4,5},{5,6},{6,7},{7,0},{8,9},{9,10},{10,1... | collective-permute-start | bytes 1179656 | tf_op jit(solution)/shard_map/ppermute | solution.py:30
  70.3 10.8 %collective-permute-start.5 = (bf16[2,192,512]{2,1,0:T(8,128)(2,1)S(1)}, bf16[2,192,512]{2,1,0:T(8,128)(2,1)S(1)}, u32[]{:S(2)}, u32[]{:S(2)}) collective-permute-start(bf16[2,192,512]{2,1,0:T(8,128)(2,1)S(1)} %collective-permute-done.4), channel_id=1, source_target_pairs={{0,1},{1,2},{2,3},{3,4},{4,5},{5,6},{6,7},{7,0},{8,9},{9,10},{10,1... | collective-permute-start | bytes 1179656 | tf_op jit(solution)/shard_map/ppermute | solution.py:30
  81.1 10.5 %collective-permute-start.6 = (bf16[2,192,512]{2,1,0:T(8,128)(2,1)S(1)}, bf16[2,192,512]{2,1,0:T(8,128)(2,1)S(1)}, u32[]{:S(2)}, u32[]{:S(2)}) collective-permute-start(bf16[2,192,512]{2,1,0:T(8,128)(2,1)S(1)} %collective-permute-done.5), channel_id=1, source_target_pairs={{0,1},{1,2},{2,3},{3,4},{4,5},{5,6},{6,7},{7,0},{8,9},{9,10},{10,1... | collective-permute-start | bytes 1179656 | tf_op jit(solution)/shard_map/ppermute | solution.py:30
  92.4 21.9 %copy-start.3 = (bf16[1024,1792]{1,0:T(8,128)(2,1)S(1)}, bf16[1024,1792]{1,0:T(8,128)(2,1)}, u32[]{:S(2)}) copy-start(bf16[1024,1792]{1,0:T(8,128)(2,1)} %param.9) | copy-start | bytes 11010052
  94.3 19.9 %collective-permute-start.9 = (bf16[2,192,1024]{2,1,0:T(8,128)(2,1)S(1)}, bf16[2,192,1024]{2,1,0:T(8,128)(2,1)S(1)}, u32[]{:S(2)}, u32[]{:S(2)}) collective-permute-start(bf16[2,192,1024]{2,1,0:T(8,128)(2,1)S(1)} %get-tuple-element.9), channel_id=1, source_target_pairs={{24,0},{16,8},{8,16},{0,24},{25,1},{17,9},{9,17},{1,25},{26,2},{18... | collective-permute-start | bytes 2359304 | tf_op jit(solution)/shard_map/ppermute | solution.py:22
  94.4 19.8 %collective-permute-start.8 = (bf16[2,192,1024]{2,1,0:T(8,128)(2,1)S(1)}, bf16[2,192,1024]{2,1,0:T(8,128)(2,1)S(1)}, u32[]{:S(2)}, u32[]{:S(2)}) collective-permute-start(bf16[2,192,1024]{2,1,0:T(8,128)(2,1)S(1)} %get-tuple-element.10), channel_id=1, source_target_pairs={{8,0},{0,8},{24,16},{16,24},{9,1},{1,9},{25,17},{17,25},{10,2},{2,... | collective-permute-start | bytes 2359304 | tf_op jit(solution)/shard_map/ppermute | solution.py:22
  95.7 47.9 %collective-permute-start.7 = (bf16[2,192,1024]{2,1,0:T(8,128)(2,1)S(1)}, bf16[2,192,1024]{2,1,0:T(8,128)(2,1)}, u32[]{:S(2)}, u32[]{:S(2)}) collective-permute-start(bf16[2,192,1024]{2,1,0:T(8,128)(2,1)S(1)} %get-tuple-element.11), channel_id=1, source_target_pairs={{16,0},{24,8},{0,16},{8,24},{17,1},{25,9},{1,17},{9,25},{18,2},{26... | collective-permute-start | bytes 2359304 | tf_op jit(solution)/shard_map/ppermute | solution.py:22
  117.1 26.4 %collective-permute-start.14 = (bf16[2,2,192,896]{3,2,0,1:T(8,128)(2,1)}, bf16[2,2,192,896]{3,2,0,1:T(8,128)(2,1)S(1)}, u32[]{:S(2)}, u32[]{:S(2)}) collective-permute-start(bf16[2,2,192,896]{3,2,0,1:T(8,128)(2,1)} %fusion.50), channel_id=1, source_target_pairs={{8,0},{0,8},{24,16},{16,24},{9,1},{1,9},{25,17},{17,25},{10,2},{2,... | collective-permute-start | bytes 4128776 | tf_op jit(solution)/shard_map/ppermute | solution.py:22
  139.2 8.9 %collective-permute-start.10 = (bf16[2,2,192,896]{3,2,1,0:T(8,128)(2,1)S(1)}, bf16[2,2,192,896]{3,2,1,0:T(8,128)(2,1)S(1)}, u32[]{:S(2)}, u32[]{:S(2)}) collective-permute-start(bf16[2,2,192,896]{3,2,1,0:T(8,128)(2,1)S(1)} %fusion.44), channel_id=1, source_target_pairs={{8,0},{0,8},{24,16},{16,24},{9,1},{1,9},{25,17},{17,25},{10,2},{2,... | collective-permute-start | bytes 4128776 | tf_op jit(solution)/shard_map/ppermute | solution.py:22
  141.1 10.7 %collective-permute-start.16 = (bf16[2,2,192,896]{3,2,0,1:T(8,128)(2,1)S(1)}, bf16[2,2,192,896]{3,2,0,1:T(8,128)(2,1)S(1)}, u32[]{:S(2)}, u32[]{:S(2)}) collective-permute-start(bf16[2,2,192,896]{3,2,0,1:T(8,128)(2,1)S(1)} %fusion.53), channel_id=1, source_target_pairs={{8,0},{0,8},{24,16},{16,24},{9,1},{1,9},{25,17},{17,25},{10,2},{2,... | collective-permute-start | bytes 4128776 | tf_op jit(solution)/shard_map/ppermute | solution.py:22
  143.4 12.9 %collective-permute-start.12 = (bf16[2,2,192,896]{3,2,0,1:T(8,128)(2,1)S(1)}, bf16[2,2,192,896]{3,2,0,1:T(8,128)(2,1)S(1)}, u32[]{:S(2)}, u32[]{:S(2)}) collective-permute-start(bf16[2,2,192,896]{3,2,0,1:T(8,128)(2,1)S(1)} %fusion.47), channel_id=1, source_target_pairs={{8,0},{0,8},{24,16},{16,24},{9,1},{1,9},{25,17},{17,25},{10,2},{2,... | collective-permute-start | bytes 4128776 | tf_op jit(solution)/shard_map/ppermute | solution.py:22
  146.6 18.4 %collective-permute-start.15 = (bf16[2,192,896]{2,1,0:T(8,128)(2,1)S(1)}, bf16[2,192,896]{2,1,0:T(8,128)(2,1)S(1)}, u32[]{:S(2)}, u32[]{:S(2)}) collective-permute-start(bf16[2,192,896]{2,1,0:T(8,128)(2,1)S(1)} %fusion.92), channel_id=1, source_target_pairs={{16,0},{24,8},{0,16},{8,24},{17,1},{25,9},{1,17},{9,25},{18,2},{26... | collective-permute-start | bytes 2064392 | tf_op jit(solution)/shard_map/ppermute | solution.py:22
  151.1 28.6 %collective-permute-start.11 = (bf16[2,192,896]{2,1,0:T(8,128)(2,1)S(1)}, bf16[2,192,896]{2,1,0:T(8,128)(2,1)S(1)}, u32[]{:S(2)}, u32[]{:S(2)}) collective-permute-start(bf16[2,192,896]{2,1,0:T(8,128)(2,1)S(1)} %fusion.90), channel_id=1, source_target_pairs={{16,0},{24,8},{0,16},{8,24},{17,1},{25,9},{1,17},{9,25},{18,2},{26... | collective-permute-start | bytes 2064392 | tf_op jit(solution)/shard_map/ppermute | solution.py:22
  154.8 39.6 %collective-permute-start.17 = (bf16[2,192,896]{2,1,0:T(8,128)(2,1)S(1)}, bf16[2,192,896]{2,1,0:T(8,128)(2,1)S(1)}, u32[]{:S(2)}, u32[]{:S(2)}) collective-permute-start(bf16[2,192,896]{2,1,0:T(8,128)(2,1)S(1)} %fusion.93), channel_id=1, source_target_pairs={{16,0},{24,8},{0,16},{8,24},{17,1},{25,9},{1,17},{9,25},{18,2},{26... | collective-permute-start | bytes 2064392 | tf_op jit(solution)/shard_map/ppermute | solution.py:22
  159.4 49.3 %collective-permute-start.13 = (bf16[2,192,896]{2,1,0:T(8,128)(2,1)S(1)}, bf16[2,192,896]{2,1,0:T(8,128)(2,1)S(1)}, u32[]{:S(2)}, u32[]{:S(2)}) collective-permute-start(bf16[2,192,896]{2,1,0:T(8,128)(2,1)S(1)} %fusion.91), channel_id=1, source_target_pairs={{16,0},{24,8},{0,16},{8,24},{17,1},{25,9},{1,17},{9,25},{18,2},{26... | collective-permute-start | bytes 2064392 | tf_op jit(solution)/shard_map/ppermute | solution.py:22
  211.8 33.1 %collective-permute-start.24 = (bf16[4,192,896]{2,1,0:T(8,128)(2,1)S(1)}, bf16[4,192,896]{2,1,0:T(8,128)(2,1)S(1)}, u32[]{:S(2)}, u32[]{:S(2)}) collective-permute-start(bf16[4,192,896]{2,1,0:T(8,128)(2,1)S(1)} %pad_maximum_fusion.6), channel_id=1, source_target_pairs={{16,0},{24,8},{0,16},{8,24},{17,1},{25,9},{1,17},{9,25},{18,2},{26... | collective-permute-start | bytes 4128776 | tf_op jit(solution)/shard_map/ppermute | solution.py:22
  213.5 60.8 %collective-permute-start.27 = (bf16[4,192,896]{2,1,0:T(8,128)(2,1)S(1)}, bf16[4,192,896]{2,1,0:T(8,128)(2,1)S(1)}, u32[]{:S(2)}, u32[]{:S(2)}) collective-permute-start(bf16[4,192,896]{2,1,0:T(8,128)(2,1)S(1)} %pad_maximum_fusion.7), channel_id=1, source_target_pairs={{16,0},{24,8},{0,16},{8,24},{17,1},{25,9},{1,17},{9,25},{18,2},{26... | collective-permute-start | bytes 4128776 | tf_op jit(solution)/shard_map/ppermute | solution.py:22
  214.1 61.5 %collective-permute-start.25 = (bf16[4,192,896]{2,1,0:T(8,128)(2,1)S(1)}, bf16[4,192,896]{2,1,0:T(8,128)(2,1)S(1)}, u32[]{:S(2)}, u32[]{:S(2)}) collective-permute-start(bf16[4,192,896]{2,1,0:T(8,128)(2,1)S(1)} %pad_maximum_fusion.6), channel_id=1, source_target_pairs={{8,0},{0,8},{24,16},{16,24},{9,1},{1,9},{25,17},{17,25},{10,2},{2,... | collective-permute-start | bytes 4128776 | tf_op jit(solution)/shard_map/ppermute | solution.py:22
  244.9 30.8 %collective-permute-start.26 = (bf16[4,192,896]{2,1,0:T(8,128)(2,1)S(1)}, bf16[4,192,896]{2,1,0:T(8,128)(2,1)S(1)}, u32[]{:S(2)}, u32[]{:S(2)}) collective-permute-start(bf16[4,192,896]{2,1,0:T(8,128)(2,1)S(1)} %collective-permute-done.24), channel_id=1, source_target_pairs={{8,0},{0,8},{24,16},{16,24},{9,1},{1,9},{25,17},{17,25},{10,2},{2,... | collective-permute-start | bytes 4128776 | tf_op jit(solution)/shard_map/ppermute | solution.py:22
  244.9 3.6 %collective-permute-start.18 = (f32[192]{0:T(256)S(1)}, f32[192]{0:T(256)S(1)}, u32[]{:S(2)}, u32[]{:S(2)}) collective-permute-start(f32[192]{0:T(256)S(1)} %add.158), channel_id=1, source_target_pairs={{1,0},{0,1},{3,2},{2,3},{5,4},{4,5},{7,6},{6,7},{9,8},{8,9},{11,10... | collective-permute-start | bytes 2312 | tf_op jit(solution)/shard_map/ppermute | solution.py:97
  248.5 3.6 %collective-permute-start.19 = (f32[192]{0:T(256)S(1)}, f32[192]{0:T(256)S(1)}, u32[]{:S(2)}, u32[]{:S(2)}) collective-permute-start(f32[192]{0:T(256)S(1)} %add.159), channel_id=1, source_target_pairs={{2,0},{3,1},{0,2},{1,3},{6,4},{7,5},{4,6},{5,7},{10,8},{11,9},{8,1... | collective-permute-start | bytes 2312 | tf_op jit(solution)/shard_map/ppermute | solution.py:97
  252.1 4.5 %collective-permute-start.20 = (f32[192]{0:T(256)S(1)}, f32[192]{0:T(256)S(1)}, u32[]{:S(2)}, u32[]{:S(2)}) collective-permute-start(f32[192]{0:T(256)S(1)} %add.160), channel_id=1, source_target_pairs={{4,0},{5,1},{6,2},{7,3},{0,4},{1,5},{2,6},{3,7},{12,8},{13,9},{14,... | collective-permute-start | bytes 2312 | tf_op jit(solution)/shard_map/ppermute | solution.py:97
  256.5 15.5 %collective-permute-start.23 = (f32[192]{0:T(256)S(1)}, f32[192]{0:T(256)S(1)}, u32[]{:S(2)}, u32[]{:S(2)}) collective-permute-start(f32[192]{0:T(256)S(1)} %add.161), channel_id=1, source_target_pairs={{24,0},{16,8},{8,16},{0,24},{25,1},{17,9},{9,17},{1,25},{26,2},{18... | collective-permute-start | bytes 2312 | tf_op jit(solution)/shard_map/ppermute | solution.py:22
  256.5 16.6 %collective-permute-start.22 = (f32[192]{0:T(256)S(1)}, f32[192]{0:T(256)S(1)}, u32[]{:S(2)}, u32[]{:S(2)}) collective-permute-start(f32[192]{0:T(256)S(1)} %add.161), channel_id=1, source_target_pairs={{8,0},{0,8},{24,16},{16,24},{9,1},{1,9},{25,17},{17,25},{10,2},{2,... | collective-permute-start | bytes 2312 | tf_op jit(solution)/shard_map/ppermute | solution.py:22
  272.1 3.6 %collective-permute-start.21 = (f32[192]{0:T(256)S(1)}, f32[192]{0:T(256)S(1)}, u32[]{:S(2)}, u32[]{:S(2)}) collective-permute-start(f32[192]{0:T(256)S(1)} %add.161), channel_id=1, source_target_pairs={{16,0},{24,8},{0,16},{8,24},{17,1},{25,9},{1,17},{9,25},{18,2},{26... | collective-permute-start | bytes 2312 | tf_op jit(solution)/shard_map/ppermute | solution.py:22
  273.2 4.0 %collective-permute-start.28 = (bf16[4,192,896]{2,1,0:T(8,128)(2,1)S(1)}, bf16[4,192,896]{2,1,0:T(8,128)(2,1)S(1)}, u32[]{:S(2)}, u32[]{:S(2)}) collective-permute-start(bf16[4,192,896]{2,1,0:T(8,128)(2,1)S(1)} %pad_maximum_fusion.7), channel_id=1, source_target_pairs={{8,0},{0,8},{24,16},{16,24},{9,1},{1,9},{25,17},{17,25},{10,2},{2,... | collective-permute-start | bytes 4128776 | tf_op jit(solution)/shard_map/ppermute | solution.py:22
  274.4 4.7 %collective-permute-start.29 = (bf16[4,192,896]{2,1,0:T(8,128)(2,1)S(1)}, bf16[4,192,896]{2,1,0:T(8,128)(2,1)S(1)}, u32[]{:S(2)}, u32[]{:S(2)}) collective-permute-start(bf16[4,192,896]{2,1,0:T(8,128)(2,1)S(1)} %collective-permute-done.27), channel_id=1, source_target_pairs={{8,0},{0,8},{24,16},{16,24},{9,1},{1,9},{25,17},{17,25},{10,2},{2,... | collective-permute-start | bytes 4128776 | tf_op jit(solution)/shard_map/ppermute | solution.py:22
  (13 other events, 88.6 us)
Sparse Core Ops, SparseCore 0:
  81.2 45.4 all-gather.1
